TPU v7x, 256 devices: a whole 4x4x8 slice. The times are simulated.
256 devices in a mesh: row: 128 (over y, z, x), head: 2 (over core).
Axes of the slice: x: 4, y: 4, z: 8, core: 2. Of those that a mesh axis runs over, the one named last changes fastest.
Arguments:
- query_single: bfloat16 [128, 384], P('row'), may hold values from -6 to 6
- key_single: bfloat16 [8192, 384], P('row'), may hold values from -6 to 6
- pair: bfloat16 [128, 8192, 128], P('row'), may hold values from -6 to 32
- query_frames: float32 [12, 128], P(None, 'row'), may hold values from -2.5 to 2.5, as said below
- key_frames: float32 [12, 8192], P(None, 'row'), may hold values from -2.5 to 2.5, as said below
- w_query: bfloat16 [384, 96], P(None, 'head'), may hold values from -0.3125 to 0.3125
- w_key: bfloat16 [384, 96], P(None, 'head'), may hold values from -0.3125 to 0.3125
- w_value: bfloat16 [384, 96], P(None, 'head'), may hold values from -0.3125 to 0.3125
- w_query_points: bfloat16 [384, 72], P(None, 'head'), may hold values from -0.3125 to 0.3125
- w_key_points: bfloat16 [384, 72], P(None, 'head'), may hold values from -0.3125 to 0.3125
- w_value_points: bfloat16 [384, 144], P(None, 'head'), may hold values from -0.3125 to 0.3125
- head_weight: float32 [6], P('head'), may hold values from -2.5 to 0.5
- bias_weight: bfloat16 [6, 128], P('head'), as said below
- w_out: bfloat16 [1056, 384], P('head'), may hold values from -0.1875 to 0.1875
- d_out: bfloat16 [128, 384], P('row'), may hold values from -24 to 24
Outputs:
- output: bfloat16 [128, 384], P('row')
- grad_query: float32 [128, 384], P('row')
- grad_keys: float32 [8192, 384], P('row')
Inputs may be any that keep to these rules, and one draw needn't show every extreme that they name: `bias_weight`: entries within -2.5 and 2.5 over the square root of 128. `query_frames`: rows 0 to 8 of each column form a rotation matrix. `key_frames`: rows 0 to 8 of each column form a rotation matrix.
All inputs are finite; a program needn't handle non-finite values.
Results may differ from a plain program's by a relative error of at most 0.012.
The roundings to bfloat16 on the way count: a program that leaves them out, or rounds other values in their place, can miss the bound.
Values may be sent and summed in bfloat16 or wider, within the bound.
A program may use at most 64 MiB of HBM per device.

v0:
```python
import math
import jax
import jax.numpy as jnp
from jax import lax
from jax.sharding import PartitionSpec as P

C = 16
PQ = 4
PV = 8
LOGIT_SCALE = math.sqrt(1.0 / 3.0)


def point_scale(points):
    return math.sqrt(2.0 / (9.0 * points))


def product(form, former, latter):
    return jnp.einsum(form, former, latter, preferred_element_type=jnp.float32)


def frame_parts(frames):
    columns = frames.shape[1]
    return (frames[:9].reshape(3, 3, columns), frames[9:12])


def rotate(vectors, rotation):
    return jnp.einsum("xyn,nhpy->nhpx", rotation, vectors, precision=lax.Precision.HIGHEST)


def unrotate(vectors, rotation):
    return jnp.einsum("xyn,nhpx->nhpy", rotation, vectors, precision=lax.Precision.HIGHEST)


def split_columns(packed, extents, axis_index):
    pieces = []
    cursor = 0
    for extent in extents:
        pieces.append(lax.slice_in_dim(packed, cursor, cursor + extent, axis=axis_index))
        cursor = cursor + extent
    return pieces


def key_side(key_single, key_frames, w_key, w_value, w_key_points, w_value_points, head_count):
    rows_k = key_single.shape[0]
    rotation, offset = frame_parts(key_frames)
    offset_rows = jnp.transpose(offset)[:, None, None, :]
    keys_b = jnp.dot(key_single, w_key, preferred_element_type=jnp.float32).astype(jnp.bfloat16)
    values_b = jnp.dot(key_single, w_value, preferred_element_type=jnp.float32).astype(jnp.bfloat16)
    local_k = jnp.dot(key_single, w_key_points, preferred_element_type=jnp.float32).reshape(
        rows_k, head_count, PQ, 3
    )
    key_pts = (rotate(local_k, rotation) + offset_rows).astype(jnp.bfloat16).reshape(rows_k, -1)
    local_v = jnp.dot(key_single, w_value_points, preferred_element_type=jnp.float32).reshape(
        rows_k, head_count, PV, 3
    )
    value_pts = (rotate(local_v, rotation) + offset_rows).astype(jnp.bfloat16).reshape(rows_k, -1)
    return (keys_b, values_b, key_pts, value_pts)


def query_pass(
    query_single,
    pair,
    query_frames,
    w_query,
    w_query_points,
    head_weight,
    bias_weight,
    w_out,
    d_out,
    keys_all,
    values_all,
    kp_all,
    vp_all,
):
    rows_q = query_single.shape[0]
    head_count = head_weight.shape[0]
    rotation, offset = frame_parts(query_frames)
    offset_rows = jnp.transpose(offset)[:, None, None, :]
    point_gain = (jax.nn.softplus(head_weight) * point_scale(PQ))[None, :, None]
    query_b = (
        jnp.dot(query_single, w_query, preferred_element_type=jnp.float32)
        .astype(jnp.bfloat16)
        .reshape(rows_q, head_count, C)
    )
    local_q = jnp.dot(query_single, w_query_points, preferred_element_type=jnp.float32).reshape(
        rows_q, head_count, PQ, 3
    )
    query_pts = (
        (rotate(local_q, rotation) + offset_rows)
        .astype(jnp.bfloat16)
        .reshape(rows_q, head_count, 3 * PQ)
    )
    query_sq = jnp.sum(jnp.square(query_pts.astype(jnp.float32)), axis=-1)
    key_sq = jnp.sum(jnp.square(kp_all.astype(jnp.float32)), axis=-1)
    pair_bias = product("hc,qkc->qhk", bias_weight, pair)
    distance = (
        query_sq[:, :, None]
        + jnp.transpose(key_sq)[None, :, :]
        - 2.0 * product("qhe,khe->qhk", query_pts, kp_all)
    )
    logits = LOGIT_SCALE * (
        product("qhc,khc->qhk", query_b, keys_all) / math.sqrt(C)
        + pair_bias
        - 0.5 * point_gain * distance
    )
    attention = jax.nn.softmax(logits, axis=-1)
    attention_b = attention.astype(jnp.bfloat16)
    attended = product("qhk,khc->qhc", attention_b, values_all)
    point_sum = product("qhk,khe->qhe", attention_b, vp_all).reshape(rows_q, head_count, PV, 3)
    pair_out = product("qhk,qkc->qhc", attention_b, pair)
    local_pts = unrotate(point_sum - offset_rows, rotation)
    lengths = jnp.sqrt(1.0 + jnp.sum(jnp.square(local_pts), axis=-1))
    features = jnp.concatenate(
        [attended, local_pts.reshape(rows_q, head_count, 3 * PV), lengths, pair_out], axis=-1
    )
    features = features.astype(jnp.bfloat16).reshape(rows_q, -1)
    output_part = jnp.dot(features, w_out, preferred_element_type=jnp.float32)
    d_features = jnp.dot(d_out, jnp.transpose(w_out), preferred_element_type=jnp.float32).reshape(
        rows_q, head_count, -1
    )
    d_attended = d_features[:, :, :C].astype(jnp.bfloat16)
    d_local = d_features[:, :, C : C + 3 * PV].reshape(rows_q, head_count, PV, 3)
    d_lengths = d_features[:, :, C + 3 * PV : C + 4 * PV]
    d_pair = d_features[:, :, C + 4 * PV :].astype(jnp.bfloat16)
    d_local = d_local + (d_lengths / lengths)[..., None] * local_pts
    d_points = rotate(d_local, rotation).astype(jnp.bfloat16).reshape(rows_q, head_count, 3 * PV)
    d_attention = (
        product("qhc,khc->qhk", d_attended, values_all)
        + product("qhe,khe->qhk", d_points, vp_all)
        + product("qhc,qkc->qhk", d_pair, pair)
    )
    row_total = jnp.sum(attention * d_attention, axis=-1, keepdims=True)
    score_b = (LOGIT_SCALE * attention * (d_attention - row_total)).astype(jnp.bfloat16)
    d_query = product("qhk,khc->qhc", score_b, keys_all) / math.sqrt(C)
    score_rows = jnp.sum(score_b.astype(jnp.float32), axis=-1)[:, :, None]
    d_qpts = point_gain * (
        product("qhk,khe->qhe", score_b, kp_all) - score_rows * query_pts.astype(jnp.float32)
    )
    d_qlocal = (
        unrotate(d_qpts.reshape(rows_q, head_count, PQ, 3), rotation)
        .astype(jnp.bfloat16)
        .reshape(rows_q, -1)
    )
    grad_part = jnp.dot(
        d_query.astype(jnp.bfloat16).reshape(rows_q, -1),
        jnp.transpose(w_query),
        preferred_element_type=jnp.float32,
    )
    grad_part = grad_part + jnp.dot(
        d_qlocal, jnp.transpose(w_query_points), preferred_element_type=jnp.float32
    )
    query_side = jnp.concatenate(
        [
            query_b.reshape(rows_q, -1),
            query_pts.reshape(rows_q, -1),
            d_attended.reshape(rows_q, -1),
            d_points.reshape(rows_q, -1),
        ],
        axis=1,
    )
    return (output_part, grad_part, query_side, attention_b, score_b)


def key_terms(attention_b, score_b, query_side, key_points, point_gain, head_count):
    count_q = query_side.shape[0]
    count_k = key_points.shape[0]
    side_parts = split_columns(
        query_side, [head_count * C, head_count * 3 * PQ, head_count * C, head_count * 3 * PV], 1
    )
    query_b = side_parts[0].reshape(count_q, head_count, C)
    query_pts = side_parts[1].reshape(count_q, head_count, 3 * PQ)
    grad_att = side_parts[2].reshape(count_q, head_count, C)
    grad_pts = side_parts[3].reshape(count_q, head_count, 3 * PV)
    d_key = product("qhk,qhc->khc", score_b, query_b) / math.sqrt(C)
    score_sum = jnp.sum(score_b.astype(jnp.float32), axis=0)
    d_kpts = point_gain * (
        product("qhk,qhe->khe", score_b, query_pts)
        - jnp.transpose(score_sum)[:, :, None] * key_points.astype(jnp.float32)
    )
    d_value = product("qhk,qhc->khc", attention_b, grad_att)
    d_vpts = product("qhk,qhe->khe", attention_b, grad_pts)
    return jnp.concatenate(
        [
            d_key.reshape(count_k, -1),
            d_value.reshape(count_k, -1),
            d_kpts.reshape(count_k, -1),
            d_vpts.reshape(count_k, -1),
        ],
        axis=1,
    )


def key_finish(key_rows, key_frames, w_key, w_value, w_key_points, w_value_points, head_count):
    rows_k = key_rows.shape[0]
    rotation, offset = frame_parts(key_frames)
    pieces = split_columns(
        key_rows, [head_count * C, head_count * C, head_count * 3 * PQ, head_count * 3 * PV], 1
    )
    kp_local = (
        unrotate(pieces[2].reshape(rows_k, head_count, PQ, 3), rotation)
        .astype(jnp.bfloat16)
        .reshape(rows_k, -1)
    )
    vp_local = (
        unrotate(pieces[3].reshape(rows_k, head_count, PV, 3), rotation)
        .astype(jnp.bfloat16)
        .reshape(rows_k, -1)
    )
    result = jnp.dot(
        pieces[0].astype(jnp.bfloat16), jnp.transpose(w_key), preferred_element_type=jnp.float32
    )
    result = result + jnp.dot(
        pieces[1].astype(jnp.bfloat16), jnp.transpose(w_value), preferred_element_type=jnp.float32
    )
    result = result + jnp.dot(
        kp_local, jnp.transpose(w_key_points), preferred_element_type=jnp.float32
    )
    return result + jnp.dot(
        vp_local, jnp.transpose(w_value_points), preferred_element_type=jnp.float32
    )


def shards(
    query_single,
    key_single,
    pair,
    query_frames,
    key_frames,
    w_query,
    w_key,
    w_value,
    w_query_points,
    w_key_points,
    w_value_points,
    head_weight,
    bias_weight,
    w_out,
    d_out,
):
    head_count = head_weight.shape[0]
    keys_b, values_b, key_pts, value_pts = key_side(
        key_single, key_frames, w_key, w_value, w_key_points, w_value_points, head_count
    )
    packed = jnp.concatenate([keys_b, values_b, key_pts, value_pts], axis=1)
    gathered = lax.all_gather(packed, "row", axis=0, tiled=True)
    total_keys = gathered.shape[0]
    pieces = split_columns(
        gathered, [head_count * C, head_count * C, head_count * 3 * PQ, head_count * 3 * PV], 1
    )
    keys_all = pieces[0].reshape(total_keys, head_count, C)
    values_all = pieces[1].reshape(total_keys, head_count, C)
    kp_all = pieces[2].reshape(total_keys, head_count, 3 * PQ)
    vp_all = pieces[3].reshape(total_keys, head_count, 3 * PV)
    output_part, grad_part, query_side, attention_b, score_b = query_pass(
        query_single,
        pair,
        query_frames,
        w_query,
        w_query_points,
        head_weight,
        bias_weight,
        w_out,
        d_out,
        keys_all,
        values_all,
        kp_all,
        vp_all,
    )
    output = lax.psum(output_part, "head").astype(jnp.bfloat16)
    point_gain = (jax.nn.softplus(head_weight) * point_scale(PQ))[None, :, None]
    scores = jnp.concatenate([attention_b, score_b], axis=1)
    rows_n = lax.axis_size("row")
    local_k = key_single.shape[0]
    scores = scores.reshape(2 * head_count, rows_n, local_k)
    scores = lax.all_to_all(scores, "row", split_axis=1, concat_axis=1, tiled=True)
    scores = jnp.transpose(scores, (1, 0, 2))
    side_all = lax.all_gather(query_side, "row", axis=0, tiled=True)
    key_rows = key_terms(
        scores[:, :head_count],
        scores[:, head_count:],
        side_all,
        key_pts.reshape(local_k, head_count, 3 * PQ),
        point_gain,
        head_count,
    )
    grad_keys_part = key_finish(
        key_rows, key_frames, w_key, w_value, w_key_points, w_value_points, head_count
    )
    grad_query, grad_keys = lax.psum((grad_part, grad_keys_part), "head")
    return (output, grad_query, grad_keys)


def solution(mesh):
    return jax.shard_map(
        shards,
        mesh=mesh,
        in_specs=(
            P("row", None),
            P("row", None),
            P("row", None, None),
            P(None, "row"),
            P(None, "row"),
            P(None, "head"),
            P(None, "head"),
            P(None, "head"),
            P(None, "head"),
            P(None, "head"),
            P(None, "head"),
            P("head"),
            P("head", None),
            P("head", None),
            P("row", None),
        ),
        out_specs=(P("row", None), P("row", None), P("row", None)),
        check_vma=False,
    )
```

profile of v0, /device:TPU:1, one launch (start us, length us, event | category | flops | bytes accessed | tf_op | source)
XLA Modules:
  0.0 621.8 jit_solution(9938110551300458424)
XLA Ops:
  10.2 7.5 %fusion.65 = f32[64,3,4,3]{2,3,1,0:T(4,128)S(1)} fusion(f32[64,3,4,3]{3,2,1,0:T(4,128)S(1)} %copy.139, f32[3,3,64,1]{0,1,3,2:T(4,128)S(1)} %copy.198), kind=kOutput, calls=%fused_computation.113 | convolution fusion | flops 82944 | bytes 20736 | tf_op jit(solution)/shard_map/xyn,nhpy->nhpx/dot_general | solution.py:27
  18.4 1.1 fusion.7
  31.2 108.1 %all-gather.3.cloned.1.call-done = bf16[8192,204]{1,0:T(8,128)(2,1)} async-done(((bf16[64,204]{1,0:T(8,128)(2,1)}), bf16[8192,204]{1,0:T(8,128)(2,1)}) %all-gather.3.cloned.1.call-update) | async-done | bytes 3342352 | tf_op jit(solution)/shard_map/all_gather | solution.py:245
  139.3 4.2 slice.77
  143.5 2.9 copy.151
  146.5 1.2 reshape.335
  149.0 4.9 fusion.59
  153.8 2.7 copy.211
  156.5 1.4 fusion.67
  157.9 1.7 fusion.63
  160.6 3.6 slice.78
  164.2 3.8 copy.212
  167.9 1.7 fusion.29
  171.0 1.6 fusion.61
  173.4 1.4 convolution_convert_fusion.6
  174.8 1.4 copy.158
  176.2 1.3 reshape.404
  177.5 1.3 reshape_reshape.14
  179.6 304.1 %all-gather = bf16[128,1,204]{2,1,0:T(2,128)(2,1)} all-gather(bf16[1,1,204]{2,1,0:T(2,128)(2,1)S(1)} %maximum_bitcast_fusion), channel_id=1, replica_groups=mesh['row'=128,'head'=2] {'row'}, dimensions={0}, use_global_device_ids=true | all-gather | bytes 52632 | tf_op jit(solution)/shard_map/all_gather | solution.py:277
  483.6 1.6 copy.163
  485.3 1.3 slice.88
  486.6 1.3 slice.87
  487.9 2.2 fusion.70
  490.1 2.6 copy.210
  492.8 1.4 fusion.50
  494.2 1.8 fusion.20
  500.3 6.1 all-to-all-start
  509.0 8.4 %all-to-all-done = bf16[128,2,192]{2,1,0:T(2,128)(2,1)S(1)} async-done(((bf16[128,2,192]{2,1,0:T(2,128)(2,1)}), bf16[128,2,192]{2,1,0:T(2,128)(2,1)S(1)}, u32[]{:S(2)}, u32[]{:S(2)}) %all-to-all-start) | async-done | bytes 98336 | tf_op jit(solution)/shard_map/all_to_all | solution.py:275
  520.6 7.4 %convolution_convert_fusion.1 = bf16[64,3,4,3]{2,3,1,0:T(4,128)(2,1)S(1)} fusion(f32[64,3,4,3]{3,2,1,0:T(4,128)S(1)} %copy.169, f32[3,3,64,1]{0,1,3,2:T(4,128)S(1)} %copy.198), kind=kOutput, calls=%fused_computation.12 | convolution fusion | flops 85248 | bytes 16128 | tf_op jit(solution)/shard_map/xyn,nhpx->nhpy/dot_general | solution.py:31
  530.2 65.1 %all-reduce = (bf16[1,384]{1,0:T(2,128)(2,1)}, f32[1,384]{1,0:T(1,128)}) all-reduce(f32[1,384]{1,0:T(1,128)S(1)} %fusion.69, f32[1,384]{1,0:T(1,128)S(1)} %add.116), channel_id=1, replica_groups=mesh['row'=128,'head'=2] {'head'}, use_global_device_ids=true, to_apply=%region_5.6 | all-reduce | flops 768 | bytes 5376 | tf_op jit(solution)/shard_map/psum | solution.py:269
  595.2 18.1 %all-reduce.3.cloned.1.call-done = f32[64,384]{1,0:T(8,128)} async-done(((f32[64,384]{1,0:T(8,128)}), f32[64,384]{1,0:T(8,128)}) %all-reduce.3.cloned.1.call-update) | async-done | bytes 98320 | tf_op jit(solution)/shard_map/psum | solution.py:289
  613.4 1.5 copy.242
  (169 shorter events, 32.3 us)
Async XLA Ops:
  7.2 150.7 %copy-start = (bf16[1,8192,128]{2,1,0:T(8,128)(2,1)S(1)}, bf16[1,8192,128]{2,1,0:T(8,128)(2,1)}, u32[]{:S(2)}) copy-start(bf16[1,8192,128]{2,1,0:T(8,128)(2,1)} %param.17) | copy-start | bytes 6291460
  7.2 10.8 %copy-start.4 = (bf16[64,384]{1,0:T(8,128)(2,1)S(1)}, bf16[64,384]{1,0:T(8,128)(2,1)}, u32[]{:S(2)}) copy-start(bf16[64,384]{1,0:T(8,128)(2,1)} %param.16) | copy-start | bytes 147460
  7.2 10.8 %copy-start.6 = (bf16[384,72]{0,1:T(8,128)(2,1)S(1)}, bf16[384,72]{0,1:T(8,128)(2,1)}, u32[]{:S(2)}) copy-start(bf16[384,72]{0,1:T(8,128)(2,1)} %param.25) | copy-start | bytes 165892
  7.2 132.1 %all-gather.3.cloned.1.call-start = ((), (), s32[]{:S(2)}) async-start(), calls=%async_computation.1 | async-start | bytes 4227072 | tf_op jit(solution)/shard_map/all_gather | solution.py:245
  8.8 13.5 %copy-start.3 = (bf16[528,384]{1,0:T(8,128)(2,1)S(1)}, bf16[528,384]{1,0:T(8,128)(2,1)}, u32[]{:S(2)}) copy-start(bf16[528,384]{1,0:T(8,128)(2,1)} %param.28) | copy-start | bytes 1216516
  8.8 13.5 %copy-start.25 = (bf16[1,384]{1,0:T(2,128)(2,1)S(1)}, bf16[1,384]{1,0:T(2,128)(2,1)}, u32[]{:S(2)}) copy-start(bf16[1,384]{1,0:T(2,128)(2,1)} %param.29) | copy-start | bytes 2308
  9.9 12.7 %copy-start.29 = (f32[12,1]{0,1:T(1,128)S(1)}, f32[12,1]{0,1:T(1,128)}, u32[]{:S(2)}) copy-start(f32[12,1]{0,1:T(1,128)} %param.18) | copy-start | bytes 148
  10.1 13.4 %copy-start.28 = (bf16[1,384]{1,0:T(2,128)(2,1)S(1)}, bf16[1,384]{1,0:T(2,128)(2,1)}, u32[]{:S(2)}) copy-start(bf16[1,384]{1,0:T(2,128)(2,1)} %param.15) | copy-start | bytes 2308
  10.1 20.5 %copy-start.30 = (f32[3]{0:T(128)S(1)}, f32[3]{0:T(128)}, u32[]{:S(2)}) copy-start(f32[3]{0:T(128)} %param.26) | copy-start | bytes 40
  22.5 121.0 %copy-start.16 = (f32[1,3,176]{2,1,0:T(4,128)}, f32[1,3,176]{2,1,0:T(4,128)S(1)}, u32[]{:S(2)}) copy-start(f32[1,3,176]{2,1,0:T(4,128)S(1)} %copy.189) | copy-start | bytes 6340
  22.6 121.0 %copy-start.18 = (bf16[1,3,176]{2,1,0:T(4,128)(2,1)}, bf16[1,3,176]{2,1,0:T(4,128)(2,1)S(1)}, u32[]{:S(2)}) copy-start(bf16[1,3,176]{2,1,0:T(4,128)(2,1)S(1)} %copy.237) | copy-start | bytes 3172
  22.7 4.6 copy-start.19
  27.2 116.3 %copy-start.24 = (bf16[48]{0:T(256)(128)(2,1)}, bf16[48]{0:T(256)(128)(2,1)S(1)}, u32[]{:S(2)}) copy-start(bf16[48]{0:T(256)(128)(2,1)S(1)} %fusion.18) | copy-start | bytes 292
  153.8 4.1 copy-start.27
  492.8 4.0 copy-start.5
  498.6 8.1 %copy-start.13 = (bf16[128,36]{0,1:T(8,128)(2,1)S(1)}, bf16[128,36]{0,1:T(8,128)(2,1)}, u32[]{:S(2)}) copy-start(bf16[128,36]{0,1:T(8,128)(2,1)} %slice.87) | copy-start | bytes 27652
  498.6 8.1 %copy-start.20 = (bf16[3,12]{1,0:T(4,128)(2,1)S(1)}, bf16[3,12]{1,0:T(4,128)(2,1)}, u32[]{:S(2)}) copy-start(bf16[3,12]{1,0:T(4,128)(2,1)} %reshape.336) | copy-start | bytes 220
  498.6 8.1 %copy-start.21 = (f32[3]{0:T(128)S(1)}, f32[3]{0:T(128)}, u32[]{:S(2)}) copy-start(f32[3]{0:T(128)} %get-tuple-element.5) | copy-start | bytes 40
  498.6 8.1 %copy-start.23 = (f32[3]{0:T(128)S(1)}, f32[3]{0:T(128)}, u32[]{:S(2)}) copy-start(f32[3]{0:T(128)} %get-tuple-element.7) | copy-start | bytes 40
  498.6 8.1 %copy-start.26 = (f32[3,1,12]{2,1,0:T(1,128)S(1)}, f32[3,1,12]{2,1,0:T(1,128)}, u32[]{:S(2)}) copy-start(f32[3,1,12]{2,1,0:T(1,128)} %fusion.25) | copy-start | bytes 436
  498.6 8.3 %copy-start.15 = (f32[3,3]{1,0:T(4,128)S(1)}, f32[3,3]{1,0:T(4,128)}, u32[]{:S(2)}) copy-start(f32[3,3]{1,0:T(4,128)} %reshape.334) | copy-start | bytes 112
  498.6 8.9 %copy-start.14 = (bf16[384,48]{0,1:T(8,128)(2,1)S(1)}, bf16[384,48]{0,1:T(8,128)(2,1)}, u32[]{:S(2)}) copy-start(bf16[384,48]{0,1:T(8,128)(2,1)} %param.20) | copy-start | bytes 110596
  498.6 9.0 %copy-start.17 = (bf16[3,8,3]{1,2,0:T(4,128)(2,1)S(1)}, bf16[3,8,3]{1,2,0:T(4,128)(2,1)}, u32[]{:S(2)}) copy-start(bf16[3,8,3]{1,2,0:T(4,128)(2,1)} %get-tuple-element.15) | copy-start | bytes 436
  499.2 20.9 %copy-start.12 = (f32[64,3,4,3]{0,1,3,2:T(4,128)S(1)}, f32[64,3,4,3]{0,1,3,2:T(4,128)}, u32[]{:S(2)}) copy-start(f32[64,3,4,3]{0,1,3,2:T(4,128)} %copy.166) | copy-start | bytes 27652
  499.2 20.9 %copy-start.22 = (f32[3]{0:T(128)S(1)}, f32[3]{0:T(128)}, u32[]{:S(2)}) copy-start(f32[3]{0:T(128)} %get-tuple-element.5) | copy-start | bytes 40
  500.3 17.1 %all-to-all-start = ((bf16[128,2,192]{2,1,0:T(2,128)(2,1)}), bf16[128,2,192]{2,1,0:T(2,128)(2,1)S(1)}, u32[]{:S(2)}, u32[]{:S(2)}) async-start(bf16[128,2,192]{2,1,0:T(2,128)(2,1)} %reshape.419), calls=%async_computation | async-start | bytes 262144 | tf_op jit(solution)/shard_map/all_to_all | solution.py:275
  506.4 107.0 %all-reduce.3.cloned.1.call-start = ((), (), s32[]{:S(2)}) async-start(), calls=%async_computation.2 | async-start | bytes 196608 | tf_op jit(solution)/shard_map/psum | solution.py:289
  508.2 20.3 %copy-start.8 = (bf16[384,48]{0,1:T(8,128)(2,1)S(1)}, bf16[384,48]{0,1:T(8,128)(2,1)}, u32[]{:S(2)}) copy-start(bf16[384,48]{0,1:T(8,128)(2,1)} %param.21) | copy-start | bytes 110596
  509.0 19.7 %copy-start.9 = (bf16[384,48]{0,1:T(8,128)(2,1)S(1)}, bf16[384,48]{0,1:T(8,128)(2,1)}, u32[]{:S(2)}) copy-start(bf16[384,48]{0,1:T(8,128)(2,1)} %param.22) | copy-start | bytes 110596
  517.5 11.4 %copy-start.11 = (bf16[384,36]{0,1:T(8,128)(2,1)S(1)}, bf16[384,36]{0,1:T(8,128)(2,1)}, u32[]{:S(2)}) copy-start(bf16[384,36]{0,1:T(8,128)(2,1)} %param.24) | copy-start | bytes 82948
  517.5 11.6 %copy-start.7 = (bf16[384,72]{0,1:T(8,128)(2,1)S(1)}, bf16[384,72]{0,1:T(8,128)(2,1)}, u32[]{:S(2)}) copy-start(bf16[384,72]{0,1:T(8,128)(2,1)} %param.25) | copy-start | bytes 165892
  518.7 11.3 %copy-start.10 = (bf16[384,36]{0,1:T(8,128)(2,1)S(1)}, bf16[384,36]{0,1:T(8,128)(2,1)}, u32[]{:S(2)}) copy-start(bf16[384,36]{0,1:T(8,128)(2,1)} %param.23) | copy-start | bytes 82948
  (2 other events, 5.8 us)
Sparse Core Ops, SparseCore 0:
  22.4 116.8 all-gather.2
  530.1 83.2 all-reduce.2
where the time goes:
time: 623 us; the launch traced here: 622 us
  blocking collectives  369 us (59%)
  waiting for transfers between devices  135 us (22%)
  local copies, waits for them, and re-layouts  50.5 us (8%)
  matrix products  40.5 us (7%)
  between operations  14.7 us (2%)
  starting transfers between devices  6.41 us (1%)
    all_gather x1, blocking collectives, shards(): side_all = lax.all_gather(query_side, 'row', axis=0, tiled=True)  304 us
    all_gather x1, waiting for transfers between devices, shards(): gathered = lax.all_gather(packed, 'row', axis=0, tiled=True)  108 us
    psum x1, blocking collectives, shards(): output = lax.psum(output_part, 'head').astype(jnp.bfloat16)  65.1 us
    slice x7, local copies, waits for them, and re-layouts, split_columns(): lax.slice_in_dim(packed, cursor, cursor + extent, axis=axis_index)  19 us
    psum x1, waiting for transfers between devices, shards(): grad_query, grad_keys = lax.psum((grad_part, grad_keys_part), 'head')  18.1 us
    dot_general x15, matrix products, product(): return jnp.einsum(form, former, latter, preferred_element_type=jnp.float32)  13.8 us
  transfers between devices with their start and end apart: 3, of which 3 were waited for; matrix products, arithmetic and copies ran while one was open for 2% of the time, Pallas kernels for 0%

commit v1 on v0

--- a/solution.py
+++ b/solution.py
@@ -266,7 +266,8 @@
         kp_all,
         vp_all,
     )
-    output = lax.psum(output_part, "head").astype(jnp.bfloat16)
+    pack_space_on_mesh = lambda vals: jnp.sum(lax.all_gather(vals, "head"), 0)
+    output = pack_space_on_mesh(output_part).astype(jnp.bfloat16)
     point_gain = (jax.nn.softplus(head_weight) * point_scale(PQ))[None, :, None]
     scores = jnp.concatenate([attention_b, score_b], axis=1)
     rows_n = lax.axis_size("row")

time: 623 us -> 625 us (level)
    all_gather x0 -> x1, blocking collectives: none -> 62.2 us  [shards(): pack_space_on_mesh = lambda vals: jnp.sum(lax.all_gather(vals, 'head'), 0)]
    psum x1, blocking collectives: 65.1 us -> 3.01 us  [shards(): grad_query, grad_keys = lax.psum((grad_part, grad_keys_part), 'head')]
where the time goes in v1:
time: 625 us; the launch traced here: 623 us
  blocking collectives  370 us (59%)
  waiting for transfers between devices  132 us (21%)
  local copies, waits for them, and re-layouts  52.9 us (8%)
  matrix products  42 us (7%)
  between operations  14.6 us (2%)
  starting transfers between devices  6.46 us (1%)
    all_gather x1, blocking collectives, shards(): side_all = lax.all_gather(query_side, 'row', axis=0, tiled=True)  305 us
    all_gather x1, waiting for transfers between devices, shards(): gathered = lax.all_gather(packed, 'row', axis=0, tiled=True)  108 us
    all_gather x1, blocking collectives, shards(): pack_space_on_mesh = lambda vals: jnp.sum(lax.all_gather(vals, 'head'), 0)  62.2 us
    slice x7, local copies, waits for them, and re-layouts, split_columns(): lax.slice_in_dim(packed, cursor, cursor + extent, axis=axis_index)  19.6 us
    psum x1, waiting for transfers between devices, shards(): grad_query, grad_keys = lax.psum((grad_part, grad_keys_part), 'head')  16.7 us
    dot_general x15, matrix products, product(): return jnp.einsum(form, former, latter, preferred_element_type=jnp.float32)  15.2 us
  transfers between devices with their start and end apart: 3, of which 3 were waited for; matrix products, arithmetic and copies ran while one was open for 2% of the time, Pallas kernels for 0%

profile of v1, /device:TPU:1, one launch (start us, length us, event | category | flops | bytes accessed | tf_op | source)
XLA Modules:
  0.0 623.2 jit_solution(12716236129625980748)
XLA Ops:
  10.2 7.5 %fusion.65 = f32[64,3,4,3]{2,3,1,0:T(4,128)S(1)} fusion(f32[64,3,4,3]{3,2,1,0:T(4,128)S(1)} %copy.139, f32[3,3,64,1]{0,1,3,2:T(4,128)S(1)} %copy.198), kind=kOutput, calls=%fused_computation.114 | convolution fusion | flops 82944 | bytes 20736 | tf_op jit(solution)/shard_map/xyn,nhpy->nhpx/dot_general | solution.py:27
  31.2 108.1 %all-gather.5.cloned.1.call-done = bf16[8192,204]{1,0:T(8,128)(2,1)} async-done(((bf16[64,204]{1,0:T(8,128)(2,1)}), bf16[8192,204]{1,0:T(8,128)(2,1)}) %all-gather.5.cloned.1.call-update) | async-done | bytes 3342352 | tf_op jit(solution)/shard_map/all_gather | solution.py:245
  139.3 4.2 slice.77
  143.5 3.0 copy.151
  149.0 4.9 fusion.59
  153.9 2.7 copy.211
  156.6 1.4 fusion.67
  158.0 1.7 fusion.63
  160.7 3.6 slice.78
  164.3 3.8 copy.212
  168.1 1.7 fusion.29
  171.1 1.6 fusion.61
  173.5 1.4 convolution_convert_fusion.6
  174.9 1.4 copy.158
  176.3 1.3 reshape.420
  177.6 1.4 reshape_reshape.14
  179.8 304.5 %all-gather.2 = bf16[128,1,204]{2,1,0:T(2,128)(2,1)} all-gather(bf16[1,1,204]{2,1,0:T(2,128)(2,1)S(1)} %maximum_bitcast_fusion), channel_id=1, replica_groups=mesh['row'=128,'head'=2] {'row'}, dimensions={0}, use_global_device_ids=true | all-gather | bytes 52632 | tf_op jit(solution)/shard_map/all_gather | solution.py:278
  484.3 1.6 copy.163
  486.0 1.3 slice.88
  487.3 1.3 slice.87
  488.6 2.2 fusion.69
  490.8 2.6 copy.210
  493.4 1.4 fusion.50
  494.9 1.8 fusion.20
  501.0 6.2 all-to-all-start
  510.0 1.3 fusion.60
  511.4 6.7 %all-to-all-done = bf16[128,2,192]{2,1,0:T(2,128)(2,1)S(1)} async-done(((bf16[128,2,192]{2,1,0:T(2,128)(2,1)}), bf16[128,2,192]{2,1,0:T(2,128)(2,1)S(1)}, u32[]{:S(2)}, u32[]{:S(2)}) %all-to-all-start) | async-done | bytes 98336 | tf_op jit(solution)/shard_map/all_to_all | solution.py:276
  522.0 7.4 %convolution_convert_fusion.1 = bf16[64,3,4,3]{2,3,1,0:T(4,128)(2,1)S(1)} fusion(f32[64,3,4,3]{3,2,1,0:T(4,128)S(1)} %copy.169, f32[3,3,64,1]{0,1,3,2:T(4,128)S(1)} %copy.198), kind=kOutput, calls=%fused_computation.12 | convolution fusion | flops 85248 | bytes 16128 | tf_op jit(solution)/shard_map/xyn,nhpx->nhpy/dot_general | solution.py:31
  532.3 62.2 %all-gather.1 = f32[2,1,384]{2,1,0:T(1,128)S(1)} all-gather(f32[1,1,384]{2,1,0:T(1,128)S(1)} %convolution_bitcast_fusion.3), channel_id=2, replica_groups=mesh['row'=128,'head'=2] {'head'}, dimensions={0}, use_global_device_ids=true | all-gather | bytes 4608 | tf_op jit(solution)/shard_map/all_gather | solution.py:269
  595.0 3.0 psum.14
  598.0 16.7 %all-reduce.2.cloned.1.call-done = f32[64,384]{1,0:T(8,128)} async-done(((f32[64,384]{1,0:T(8,128)}), f32[64,384]{1,0:T(8,128)}) %all-reduce.2.cloned.1.call-update) | async-done | bytes 98320 | tf_op jit(solution)/shard_map/psum | solution.py:290
  614.8 1.5 copy.242
  (172 shorter events, 37.0 us)
Async XLA Ops:
  7.2 150.8 %copy-start = (bf16[1,8192,128]{2,1,0:T(8,128)(2,1)S(1)}, bf16[1,8192,128]{2,1,0:T(8,128)(2,1)}, u32[]{:S(2)}) copy-start(bf16[1,8192,128]{2,1,0:T(8,128)(2,1)} %param.17) | copy-start | bytes 6291460
  7.2 10.8 %copy-start.4 = (bf16[64,384]{1,0:T(8,128)(2,1)S(1)}, bf16[64,384]{1,0:T(8,128)(2,1)}, u32[]{:S(2)}) copy-start(bf16[64,384]{1,0:T(8,128)(2,1)} %param.16) | copy-start | bytes 147460
  7.2 10.8 %copy-start.6 = (bf16[384,72]{0,1:T(8,128)(2,1)S(1)}, bf16[384,72]{0,1:T(8,128)(2,1)}, u32[]{:S(2)}) copy-start(bf16[384,72]{0,1:T(8,128)(2,1)} %param.25) | copy-start | bytes 165892
  7.2 132.1 %all-gather.5.cloned.1.call-start = ((), (), s32[]{:S(2)}) async-start(), calls=%async_computation.1 | async-start | bytes 4227072 | tf_op jit(solution)/shard_map/all_gather | solution.py:245
  8.8 13.5 %copy-start.3 = (bf16[528,384]{1,0:T(8,128)(2,1)S(1)}, bf16[528,384]{1,0:T(8,128)(2,1)}, u32[]{:S(2)}) copy-start(bf16[528,384]{1,0:T(8,128)(2,1)} %param.28) | copy-start | bytes 1216516
  8.8 13.5 %copy-start.25 = (bf16[1,384]{1,0:T(2,128)(2,1)S(1)}, bf16[1,384]{1,0:T(2,128)(2,1)}, u32[]{:S(2)}) copy-start(bf16[1,384]{1,0:T(2,128)(2,1)} %param.29) | copy-start | bytes 2308
  9.9 12.7 %copy-start.29 = (f32[12,1]{0,1:T(1,128)S(1)}, f32[12,1]{0,1:T(1,128)}, u32[]{:S(2)}) copy-start(f32[12,1]{0,1:T(1,128)} %param.18) | copy-start | bytes 148
  10.1 13.4 %copy-start.28 = (bf16[1,384]{1,0:T(2,128)(2,1)S(1)}, bf16[1,384]{1,0:T(2,128)(2,1)}, u32[]{:S(2)}) copy-start(bf16[1,384]{1,0:T(2,128)(2,1)} %param.15) | copy-start | bytes 2308
  10.1 20.5 %copy-start.30 = (f32[3]{0:T(128)S(1)}, f32[3]{0:T(128)}, u32[]{:S(2)}) copy-start(f32[3]{0:T(128)} %param.26) | copy-start | bytes 40
  22.5 121.0 %copy-start.16 = (f32[1,3,176]{2,1,0:T(4,128)}, f32[1,3,176]{2,1,0:T(4,128)S(1)}, u32[]{:S(2)}) copy-start(f32[1,3,176]{2,1,0:T(4,128)S(1)} %copy.189) | copy-start | bytes 6340
  22.6 121.0 %copy-start.18 = (bf16[1,3,176]{2,1,0:T(4,128)(2,1)}, bf16[1,3,176]{2,1,0:T(4,128)(2,1)S(1)}, u32[]{:S(2)}) copy-start(bf16[1,3,176]{2,1,0:T(4,128)(2,1)S(1)} %copy.237) | copy-start | bytes 3172
  22.7 4.5 copy-start.19
  27.2 116.3 %copy-start.24 = (bf16[48]{0:T(256)(128)(2,1)}, bf16[48]{0:T(256)(128)(2,1)S(1)}, u32[]{:S(2)}) copy-start(bf16[48]{0:T(256)(128)(2,1)S(1)} %fusion.18) | copy-start | bytes 292
  153.9 4.1 copy-start.27
  493.4 4.0 copy-start.5
  499.2 8.1 %copy-start.13 = (bf16[128,36]{0,1:T(8,128)(2,1)S(1)}, bf16[128,36]{0,1:T(8,128)(2,1)}, u32[]{:S(2)}) copy-start(bf16[128,36]{0,1:T(8,128)(2,1)} %slice.87) | copy-start | bytes 27652
  499.2 8.8 %copy-start.21 = (bf16[3,12]{1,0:T(4,128)(2,1)S(1)}, bf16[3,12]{1,0:T(4,128)(2,1)}, u32[]{:S(2)}) copy-start(bf16[3,12]{1,0:T(4,128)(2,1)} %reshape.347) | copy-start | bytes 220
  499.2 8.8 %copy-start.22 = (f32[3]{0:T(128)S(1)}, f32[3]{0:T(128)}, u32[]{:S(2)}) copy-start(f32[3]{0:T(128)} %get-tuple-element.3) | copy-start | bytes 40
  499.3 8.8 %copy-start.23 = (f32[3]{0:T(128)S(1)}, f32[3]{0:T(128)}, u32[]{:S(2)}) copy-start(f32[3]{0:T(128)} %get-tuple-element.5) | copy-start | bytes 40
  499.3 8.7 %copy-start.26 = (f32[3,1,12]{2,1,0:T(1,128)S(1)}, f32[3,1,12]{2,1,0:T(1,128)}, u32[]{:S(2)}) copy-start(f32[3,1,12]{2,1,0:T(1,128)} %fusion.25) | copy-start | bytes 436
  499.3 8.9 %copy-start.15 = (f32[3,3]{1,0:T(4,128)S(1)}, f32[3,3]{1,0:T(4,128)}, u32[]{:S(2)}) copy-start(f32[3,3]{1,0:T(4,128)} %reshape.345) | copy-start | bytes 112
  499.3 9.4 %copy-start.10 = (bf16[384,36]{0,1:T(8,128)(2,1)S(1)}, bf16[384,36]{0,1:T(8,128)(2,1)}, u32[]{:S(2)}) copy-start(bf16[384,36]{0,1:T(8,128)(2,1)} %param.23) | copy-start | bytes 82948
  499.3 9.6 %copy-start.14 = (bf16[384,48]{0,1:T(8,128)(2,1)S(1)}, bf16[384,48]{0,1:T(8,128)(2,1)}, u32[]{:S(2)}) copy-start(bf16[384,48]{0,1:T(8,128)(2,1)} %param.20) | copy-start | bytes 110596
  499.3 10.3 %copy-start.17 = (bf16[3,8,3]{1,2,0:T(4,128)(2,1)S(1)}, bf16[3,8,3]{1,2,0:T(4,128)(2,1)}, u32[]{:S(2)}) copy-start(bf16[3,8,3]{1,2,0:T(4,128)(2,1)} %get-tuple-element.13) | copy-start | bytes 436
  501.0 17.1 %all-to-all-start = ((bf16[128,2,192]{2,1,0:T(2,128)(2,1)}), bf16[128,2,192]{2,1,0:T(2,128)(2,1)S(1)}, u32[]{:S(2)}, u32[]{:S(2)}) async-start(bf16[128,2,192]{2,1,0:T(2,128)(2,1)} %reshape.435), calls=%async_computation | async-start | bytes 262144 | tf_op jit(solution)/shard_map/all_to_all | solution.py:276
  507.1 107.7 %all-reduce.2.cloned.1.call-start = ((), (), s32[]{:S(2)}) async-start(), calls=%async_computation.2 | async-start | bytes 196608 | tf_op jit(solution)/shard_map/psum | solution.py:290
  509.8 20.9 %copy-start.8 = (bf16[384,48]{0,1:T(8,128)(2,1)S(1)}, bf16[384,48]{0,1:T(8,128)(2,1)}, u32[]{:S(2)}) copy-start(bf16[384,48]{0,1:T(8,128)(2,1)} %param.21) | copy-start | bytes 110596
  511.4 19.5 %copy-start.9 = (bf16[384,48]{0,1:T(8,128)(2,1)S(1)}, bf16[384,48]{0,1:T(8,128)(2,1)}, u32[]{:S(2)}) copy-start(bf16[384,48]{0,1:T(8,128)(2,1)} %param.22) | copy-start | bytes 110596
  518.2 12.8 %copy-start.11 = (bf16[384,36]{0,1:T(8,128)(2,1)S(1)}, bf16[384,36]{0,1:T(8,128)(2,1)}, u32[]{:S(2)}) copy-start(bf16[384,36]{0,1:T(8,128)(2,1)} %param.24) | copy-start | bytes 82948
  518.3 13.0 %copy-start.7 = (bf16[384,72]{0,1:T(8,128)(2,1)S(1)}, bf16[384,72]{0,1:T(8,128)(2,1)}, u32[]{:S(2)}) copy-start(bf16[384,72]{0,1:T(8,128)(2,1)} %param.25) | copy-start | bytes 165892
  518.4 11.2 %copy-start.12 = (bf16[128,48]{0,1:T(8,128)(2,1)S(1)}, bf16[128,48]{0,1:T(8,128)(2,1)}, u32[]{:S(2)}) copy-start(bf16[128,48]{0,1:T(8,128)(2,1)} %get-tuple-element.11) | copy-start | bytes 36868
  519.7 75.4 %copy-start.20 = (f32[1,384]{1,0:T(1,128)S(1)}, f32[1,384]{1,0:T(1,128)}, u32[]{:S(2)}) copy-start(f32[1,384]{1,0:T(1,128)} %add.114) | copy-start | bytes 4612
  (2 other events, 5.8 us)
Sparse Core Ops, SparseCore 0:
  22.4 116.8 all-gather.4
  532.3 82.4 all-reduce.1
